TPU v7x, 256 devices: a whole 4x4x8 slice. The times are simulated.
256 devices in a mesh: view: 16 (over y, x), scene: 16 (over z, core).
Axes of the slice: x: 4, y: 4, z: 8, core: 2. Of those that a mesh axis runs over, the one named last changes fastest.
Arguments:
- params: float32 [14, 262144], P(None, 'scene'), may hold values from -3 to 3
- pixel_basis: float32 [512, 13, 256], P('view'), may hold values from -6 to 6
- tile_blocks: int32 [512, 16, 2], P('view', 'scene'), may hold values from 0 to 127
- depth_rank: int32 [512, 32], P('view'), may hold values from 0 to 31, each once within a row
- target: float32 [512, 256], P('view'), may hold values from -0.3 to 0.3
Outputs:
- step: float32 [14, 262144], P(None, 'scene')
- residual: float32 [512, 256], P('view')
Inputs may be any that keep to these rules, and one draw needn't show every extreme that they name: `tile_blocks`: index of a block among the 128 blocks held by the owner named by the second dimension; a tile may list a block more than once. `depth_rank`: each row is a permutation of the 32 slots; a lower rank lies in front.
All inputs are finite; a program needn't handle non-finite values.
Results may differ from a plain program's by a relative error of at most 0.0003.
Values sent between devices are 32-bit elements; how exact they have to be, the bound alone decides.
A program may use at most 128 MiB of HBM per device.

v0:
```python
import jax
import jax.numpy as jnp
from jax import lax
from jax.sharding import PartitionSpec as P

BLOCK_SIZE = 128
ITERS = 3
alpha_max = 0.004
damping = 0.1
ridge_term = 0.0001
highest = lax.Precision.HIGHEST


def local(params, pixel_basis, tile_blocks, depth_rank, target):
    param_count = params.shape[0]
    tile_count = pixel_basis.shape[0]
    owned_slots = tile_blocks.shape[2]
    block_width = BLOCK_SIZE
    blocks = params.shape[1] // block_width
    param_blocks = params.reshape(param_count, blocks, block_width)
    pair_ids = tile_blocks.reshape(tile_count * owned_slots)
    onehot = (pair_ids[:, None] == jnp.arange(blocks, dtype=jnp.int32)[None, :]).astype(jnp.float32)
    position = lax.broadcasted_iota(jnp.int32, (block_width, block_width), 0)
    later_index = lax.broadcasted_iota(jnp.int32, (block_width, block_width), 1)
    strict = (position < later_index).astype(jnp.float32)
    pieces = jnp.take(param_blocks, pair_ids, axis=1).reshape(
        param_count, tile_count, owned_slots, block_width
    )
    logits = jnp.einsum("tcq,ctjg->tjqg", pixel_basis, pieces[: param_count - 1], precision=highest)
    opacity = alpha_max * jax.nn.sigmoid(logits)
    log_keep = jnp.log1p(-opacity)
    inner_log = jnp.einsum("tjqg,gh->tjqh", log_keep, strict, precision=highest)
    colour, opacity, log_keep, inner_log = (pieces[param_count - 1], opacity, log_keep, inner_log)
    block_log = jnp.sum(log_keep, axis=3)
    all_logs = lax.all_gather(block_log, "scene", axis=1, tiled=True)
    own_rank = lax.dynamic_slice_in_dim(
        depth_rank, lax.axis_index("scene") * owned_slots, owned_slots, 1
    )
    earlier = (depth_rank[:, None, :] < own_rank[:, :, None]).astype(jnp.float32)
    front_log = jnp.einsum("tjl,tlq->tjq", earlier, all_logs, precision=highest)
    weight_now = jnp.exp(front_log[:, :, :, None] + inner_log) * opacity
    slope_now = weight_now * colour[:, :, None, :] * (1.0 - opacity / alpha_max)
    weight = weight_now
    slopes = slope_now
    render_part = jnp.sum(weight * colour[:, :, None, :], axis=(1, 3))
    render = lax.psum(render_part, "scene")
    residual = render - target

    def to_blocks(feature, colour_term):
        stacked = jnp.concatenate([feature, colour_term[None]], axis=0)
        stacked = stacked.reshape(param_count, tile_count * owned_slots, block_width)
        return jnp.einsum("cpg,pb->cbg", stacked, onehot, precision=highest)

    def transpose_apply(weight_now, slope_now, pixel_vec):
        spread = pixel_vec[:, None, :, None]
        feature = jnp.einsum("tcq,tjqg->ctjg", pixel_basis, slope_now * spread, precision=highest)
        colour_term = jnp.sum(weight_now * spread, axis=2)
        return to_blocks(feature, colour_term)

    grad_part = transpose_apply(weight, slopes, residual)
    diag_feature = jnp.einsum(
        "tcq,tjqg->ctjg", pixel_basis * pixel_basis, slopes * slopes, precision=highest
    )
    diag_part = to_blocks(diag_feature, jnp.sum(weight * weight, axis=2))
    gradient, curv_diag = lax.psum((grad_part, diag_part), "view")

    def inner_sum(first_vec, second_vec):
        local_sum = jnp.sum(first_vec * second_vec)
        return lax.psum(local_sum, "scene")

    precondition = (1.0 + damping) * curv_diag + ridge_term
    solution = jnp.zeros_like(gradient)
    remainder = -gradient
    scaled = remainder / precondition
    direction = scaled
    rho_now = inner_sum(remainder, scaled)
    for iteration in range(ITERS):
        full_dir = direction
        forward_pieces = jnp.take(full_dir, pair_ids, axis=1).reshape(
            param_count, tile_count, owned_slots, block_width
        )
        projected = jnp.einsum(
            "tcq,ctjg->tjqg", pixel_basis, forward_pieces[: param_count - 1], precision=highest
        )
        partial_value = jnp.sum(
            slopes * projected + weight * forward_pieces[param_count - 1][:, :, None, :],
            axis=(1, 3),
        )
        curvature_pixel_vec = lax.psum(partial_value, "scene")
        curvature_partial_value = transpose_apply(weight, slopes, curvature_pixel_vec)
        reduced = lax.psum(curvature_partial_value, "view")
        image_dir = reduced + (damping * curv_diag + ridge_term) * direction
        step_size = rho_now / inner_sum(direction, image_dir)
        solution = solution + step_size * direction
        if iteration + 1 < ITERS:
            remainder = remainder - step_size * image_dir
            scaled = remainder / precondition
            rho_next = inner_sum(remainder, scaled)
            direction = scaled + rho_next / rho_now * direction
            rho_now = rho_next
    return (solution.reshape(param_count, blocks * block_width), residual)


def solution(mesh):
    in_specs = (
        P(None, "scene"),
        P("view", None, None),
        P("view", "scene", None),
        P("view", None),
        P("view", None),
    )
    out_specs = (P(None, "scene"), P("view", None))
    return jax.shard_map(local, mesh=mesh, in_specs=in_specs, out_specs=out_specs, check_vma=False)
```

profile of v0, /device:TPU:1, one launch (start us, length us, event | category | flops | bytes accessed | tf_op | source)
XLA Modules:
  0.0 938.0 jit_solution(4138145236380710642)
XLA Ops:
  11.0 14.0 %fusion.19 = (f32[32,2,256]{2,1,0:T(2,128)S(1)}, f32[32,2,128,256]{3,2,1,0:T(8,128)}) fusion(f32[13,32,2,128]{3,0,2,1:T(8,128)S(1)} %bitcast.140, f32[32,13,256,1]{2,0,1,3:T(8,128)} %bitcast.120), kind=kOutput, calls=%fused_computation.35 | convolution fusion | flops 339722240 | bytes 9306112 | tf_op jit(solution)/shard_map/tcq,ctjg->tjqg/dot_general | solution.py:29
  26.1 42.5 %all-gather.2.cloned.1.call-done = f32[32,32,256]{2,0,1:T(8,128)} async-done(((f32[32,2,256]{2,0,1:T(8,128)}), f32[32,32,256]{2,0,1:T(8,128)}) %all-gather.2.cloned.1.call-update) | async-done | bytes 1048592 | tf_op jit(solution)/shard_map/all_gather | solution.py:35
  70.8 18.9 %bitcast_multiply_fusion.3 = (f32[32,2,256,128]{2,3,1,0:T(8,128)}, f32[32,256]{1,0:T(8,128)S(1)}, f32[32,2,256,128]{2,3,1,0:T(8,128)}) fusion(f32[32,2,128,256]{3,2,1,0:T(8,128)} %get-tuple-element.14, f32[32,2,128]{2,1,0:T(2,128)S(1)} %bitcast.146, f32[32,2,256]{2,1,0:T(2,128)S(1)} %fusion.27), kind=kOutput, calls=%fused_computation.13 | convolution fusion | flops 3240108032 | bytes 25296896 | tf_op jit(solution)/shard_map/tjqg,gh->tjqh/dot_general | solution.py:32
  89.8 43.5 %psum.105 = f32[32,256]{1,0:T(8,128)S(1)} all-reduce(f32[32,256]{1,0:T(8,128)S(1)} %get-tuple-element.12), channel_id=1, replica_groups=mesh['view'=16,'scene'=16] {'scene'}, use_global_device_ids=true, to_apply=%region_2.4 | all-reduce | flops 8192 | bytes 65536 | tf_op jit(solution)/shard_map/psum | solution.py:46
  133.3 10.4 %fusion.15 = f32[32,2,128,13]{2,3,1,0:T(8,128)S(1)} fusion(f32[32,2,256,128]{2,3,1,0:T(8,128)} %get-tuple-element.11, f32[32,256]{1,0:T(8,128)S(1)} %sub.13, f32[32,13,256,1]{2,0,1,3:T(8,128)S(1)} %bitcast.121), kind=kOutput, calls=%fused_computation.30 | convolution fusion | flops 329252864 | bytes 9273344 | tf_op jit(solution)/shard_map/tcq,tjqg->ctjg/dot_general | solution.py:56
  143.9 2.3 multiply_reduce_fusion.4
  146.3 7.5 fusion.13
  157.1 101.0 %all-reduce.13.cloned.1.call-done = (f32[14,128,128]{2,1,0:T(8,128)}, f32[14,128,128]{2,1,0:T(8,128)}) async-done(((f32[14,128,128]{2,1,0:T(8,128)}, f32[14,128,128]{2,1,0:T(8,128)}), (f32[14,128,128]{2,1,0:T(8,128)}, f32[14,128,128]{2,1,0:T(8,128)})) %all-reduce.13.cloned.1.call-update) | async-done | bytes 1835024 | tf_op jit(solution)/shard_map/psum | solution.py:65
  261.2 12.3 %fusion.5 = f32[32,256]{1,0:T(8,128)S(1)} fusion(f32[32,2,256,128]{2,3,1,0:T(8,128)} %get-tuple-element.11, f32[32,2,256,128]{2,3,1,0:T(8,128)} %get-tuple-element.15, f32[32,2,128]{2,1,0:T(2,128)S(1)} %bitcast.147, f32[13,32,2,128]{3,0,2,1:T(8,128)S(1)} %bitcast.131, f32[32,13,256,1]{2,0,1,3:T(8,128)S(1)} %bitcast.122), kind=kOutput, calls=%fused_computation.12 | convolution fusion | flops 335536128 | bytes 17694720 | tf_op jit(solution)/shard_map/tcq,ctjg->tjqg/dot_general | solution.py:82
  273.5 45.5 %psum.109 = f32[32,256]{1,0:T(8,128)S(1)} all-reduce(f32[32,256]{1,0:T(8,128)S(1)} %fusion.5), channel_id=1, replica_groups=mesh['view'=16,'scene'=16] {'scene'}, use_global_device_ids=true, to_apply=%region_10.12 | all-reduce | flops 8192 | bytes 65536 | tf_op jit(solution)/shard_map/psum | solution.py:89
  318.9 10.0 %fusion.11 = f32[32,2,128,13]{2,3,1,0:T(8,128)S(1)} fusion(f32[32,2,256,128]{2,3,1,0:T(8,128)} %get-tuple-element.11, f32[32,256]{1,0:T(8,128)S(1)} %psum.109, f32[32,13,256,1]{2,0,1,3:T(8,128)S(1)} %bitcast.123), kind=kOutput, calls=%fused_computation.24 | convolution fusion | flops 329252864 | bytes 9273344 | tf_op jit(solution)/shard_map/tcq,tjqg->ctjg/dot_general | solution.py:56
  328.9 4.6 multiply_reduce_fusion.2
  335.2 96.4 %all-reduce.7.cloned.1.call-done = f32[14,128,128]{2,1,0:T(8,128)} async-done(((f32[14,128,128]{2,1,0:T(8,128)}), f32[14,128,128]{2,1,0:T(8,128)}) %all-reduce.7.cloned.1.call-update) | async-done | bytes 917520 | tf_op jit(solution)/shard_map/psum | solution.py:91
  433.9 26.2 %all-reduce = (f32[]{:T(128)}, f32[]{:T(128)}) all-reduce(f32[]{:T(128)} %get-tuple-element.6, f32[]{:T(128)} %get-tuple-element.5), channel_id=1, replica_groups=mesh['view'=16,'scene'=16] {'scene'}, use_global_device_ids=true, to_apply=%region_8.10 | all-reduce | flops 2 | bytes 16 | tf_op jit(solution)/shard_map/psum | solution.py:69
  463.7 25.1 %psum.112 = f32[]{:T(128)} all-reduce(f32[]{:T(128)} %multiply_reduce_fusion.9), channel_id=1, replica_groups=mesh['view'=16,'scene'=16] {'scene'}, use_global_device_ids=true, to_apply=%region_16.18 | all-reduce | flops 1 | bytes 8 | tf_op jit(solution)/shard_map/psum | solution.py:69
  493.3 2.6 gather_fusion.2
  497.1 12.1 %fusion.3 = f32[32,256]{1,0:T(8,128)S(1)} fusion(f32[32,2,256,128]{2,3,1,0:T(8,128)} %get-tuple-element.11, f32[32,2,256,128]{2,3,1,0:T(8,128)} %get-tuple-element.15, f32[32,2,128]{2,1,0:T(2,128)S(1)} %bitcast.148, f32[13,32,2,128]{3,0,2,1:T(8,128)S(1)} %bitcast.132, f32[32,13,256,1]{2,0,1,3:T(8,128)S(1)} %bitcast.124), kind=kOutput, calls=%fused_computation.9 | convolution fusion | flops 335536128 | bytes 17694720 | tf_op jit(solution)/shard_map/tcq,ctjg->tjqg/dot_general | solution.py:82
  509.2 42.8 %psum.113 = f32[32,256]{1,0:T(8,128)S(1)} all-reduce(f32[32,256]{1,0:T(8,128)S(1)} %fusion.3), channel_id=1, replica_groups=mesh['view'=16,'scene'=16] {'scene'}, use_global_device_ids=true, to_apply=%region_18.20 | all-reduce | flops 8192 | bytes 65536 | tf_op jit(solution)/shard_map/psum | solution.py:89
  552.0 9.8 %fusion.9 = f32[32,2,128,13]{2,3,1,0:T(8,128)S(1)} fusion(f32[32,2,256,128]{2,3,1,0:T(8,128)} %get-tuple-element.11, f32[32,256]{1,0:T(8,128)S(1)} %psum.113, f32[32,13,256,1]{2,0,1,3:T(8,128)S(1)} %bitcast.125), kind=kOutput, calls=%fused_computation.21 | convolution fusion | flops 329252864 | bytes 9273344 | tf_op jit(solution)/shard_map/tcq,tjqg->ctjg/dot_general | solution.py:56
  561.8 4.6 multiply_reduce_fusion.1
  568.2 95.9 %all-reduce.9.cloned.1.call-done = f32[14,128,128]{2,1,0:T(8,128)} async-done(((f32[14,128,128]{2,1,0:T(8,128)}), f32[14,128,128]{2,1,0:T(8,128)}) %all-reduce.9.cloned.1.call-update) | async-done | bytes 917520 | tf_op jit(solution)/shard_map/psum | solution.py:91
  666.2 26.2 %psum.115 = f32[]{:T(128)} all-reduce(f32[]{:T(128)} %multiply_reduce_fusion.8), channel_id=1, replica_groups=mesh['view'=16,'scene'=16] {'scene'}, use_global_device_ids=true, to_apply=%region_22.24 | all-reduce | flops 1 | bytes 8 | tf_op jit(solution)/shard_map/psum | solution.py:69
  693.6 2.6 multiply_reduce_fusion.7
  696.2 25.2 %psum.116 = f32[]{:T(128)} all-reduce(f32[]{:T(128)} %multiply_reduce_fusion.7), channel_id=1, replica_groups=mesh['view'=16,'scene'=16] {'scene'}, use_global_device_ids=true, to_apply=%region_24.26 | all-reduce | flops 1 | bytes 8 | tf_op jit(solution)/shard_map/psum | solution.py:69
  727.2 2.6 gather_fusion.3
  731.0 12.1 %fusion.1 = f32[32,256]{1,0:T(8,128)S(1)} fusion(f32[32,2,256,128]{2,3,1,0:T(8,128)} %get-tuple-element.11, f32[32,2,256,128]{2,3,1,0:T(8,128)} %get-tuple-element.15, f32[32,2,128]{2,1,0:T(2,128)S(1)} %bitcast.149, f32[13,32,2,128]{3,0,2,1:T(8,128)S(1)} %bitcast.130, f32[32,13,256,1]{2,0,1,3:T(8,128)S(1)} %bitcast.126), kind=kOutput, calls=%fused_computation.6 | convolution fusion | flops 335536128 | bytes 17694720 | tf_op jit(solution)/shard_map/tcq,ctjg->tjqg/dot_general | solution.py:82
  743.1 42.8 %psum.117 = f32[32,256]{1,0:T(8,128)S(1)} all-reduce(f32[32,256]{1,0:T(8,128)S(1)} %fusion.1), channel_id=1, replica_groups=mesh['view'=16,'scene'=16] {'scene'}, use_global_device_ids=true, to_apply=%region_26.28 | all-reduce | flops 8192 | bytes 65536 | tf_op jit(solution)/shard_map/psum | solution.py:89
  785.9 9.8 %fusion.7 = f32[32,2,128,13]{2,3,1,0:T(8,128)S(1)} fusion(f32[32,2,256,128]{2,3,1,0:T(8,128)} %get-tuple-element.11, f32[32,256]{1,0:T(8,128)S(1)} %psum.117, f32[32,13,256,1]{2,0,1,3:T(8,128)S(1)} %bitcast.127), kind=kOutput, calls=%fused_computation.18 | convolution fusion | flops 329252864 | bytes 9273344 | tf_op jit(solution)/shard_map/tcq,tjqg->ctjg/dot_general | solution.py:56
  795.8 4.6 multiply_reduce_fusion
  802.1 96.0 %all-reduce.11.cloned.1.call-done = f32[14,128,128]{2,1,0:T(8,128)} async-done(((f32[14,128,128]{2,1,0:T(8,128)}), f32[14,128,128]{2,1,0:T(8,128)}) %all-reduce.11.cloned.1.call-update) | async-done | bytes 917520 | tf_op jit(solution)/shard_map/psum | solution.py:91
  898.1 2.3 multiply_reduce_fusion.6
  900.4 26.2 %psum.119 = f32[]{:T(128)} all-reduce(f32[]{:T(128)} %multiply_reduce_fusion.6), channel_id=1, replica_groups=mesh['view'=16,'scene'=16] {'scene'}, use_global_device_ids=true, to_apply=%region_30.32 | all-reduce | flops 1 | bytes 8 | tf_op jit(solution)/shard_map/psum | solution.py:69
  (76 shorter events, 38.3 us)
Async XLA Ops:
  7.2 61.4 %all-gather.2.cloned.1.call-start = ((), (), s32[]{:S(2)}) async-start(), calls=%async_computation | async-start | bytes 1114112 | tf_op jit(solution)/shard_map/all_gather | solution.py:35
  11.0 15.0 %copy-start.6 = (s32[32,32]{1,0:T(8,128)S(1)}, s32[32,32]{1,0:T(8,128)}, u32[]{:S(2)}) copy-start(s32[32,32]{1,0:T(8,128)} %param.10) | copy-start | bytes 12292
  11.0 15.1 %copy-start.3 = (f32[32,13,256]{2,0,1:T(8,128)S(1)}, f32[32,13,256]{2,0,1:T(8,128)}, u32[]{:S(2)}) copy-start(f32[32,13,256]{2,0,1:T(8,128)} %param.8) | copy-start | bytes 1277956
  25.7 232.5 %all-reduce.13.cloned.1.call-start = ((), (), s32[]{:S(2)}) async-start(), calls=%async_computation.4 | async-start | bytes 3670016 | tf_op jit(solution)/shard_map/psum | solution.py:65
  70.8 62.5 %copy-start.7 = (f32[32,256]{1,0:T(8,128)S(1)}, f32[32,256]{1,0:T(8,128)}, u32[]{:S(2)}) copy-start(f32[32,256]{1,0:T(8,128)} %param.11) | copy-start | bytes 98308
  133.3 10.6 %copy-start = (f32[32,2,256,128]{2,3,1,0:T(8,128)S(1)}, f32[32,2,256,128]{2,3,1,0:T(8,128)}, u32[]{:S(2)}) copy-start(f32[32,2,256,128]{2,3,1,0:T(8,128)} %get-tuple-element.15) | copy-start | bytes 25165828
  133.3 12.9 %copy-start.5 = (f32[32,256]{1,0:T(8,128)}, f32[32,256]{1,0:T(8,128)S(1)}, u32[]{:S(2)}) copy-start(f32[32,256]{1,0:T(8,128)S(1)} %sub.13) | copy-start | bytes 98308
  133.3 12.9 %slice-start = ((s8[8388608]{0:T(1024)(128)(4,1)}), s8[4194304]{0:T(1024)(128)(4,1)S(1)}, s32[]{:S(2)}) async-start(s8[8388608]{0:T(1024)(128)(4,1)} %bitcast.118), calls=%async_computation.5 | async-start | bytes 8388608
  133.3 12.9 %slice-start.1 = ((s8[8388608]{0:T(1024)(128)(4,1)}), s8[4194304]{0:T(1024)(128)(4,1)S(1)}, s32[]{:S(2)}) async-start(s8[8388608]{0:T(1024)(128)(4,1)} %bitcast.118), calls=%async_computation.6 | async-start | bytes 8388608
  157.1 274.6 %all-reduce.7.cloned.1.call-start = ((), (), s32[]{:S(2)}) async-start(), calls=%async_computation.1 | async-start | bytes 1835008 | tf_op jit(solution)/shard_map/psum | solution.py:91
  318.9 112.7 %copy-start.1 = (f32[14,128,128]{2,1,0:T(8,128)S(1)}, f32[14,128,128]{2,1,0:T(8,128)}, u32[]{:S(2)}) copy-start(f32[14,128,128]{2,1,0:T(8,128)} %get-tuple-element.9) | copy-start | bytes 2752516
  318.9 112.7 %copy-start.2 = (f32[14,128,128]{2,1,0:T(8,128)S(1)}, f32[14,128,128]{2,1,0:T(8,128)}, u32[]{:S(2)}) copy-start(f32[14,128,128]{2,1,0:T(8,128)} %get-tuple-element.10) | copy-start | bytes 2752516
  335.2 328.9 %all-reduce.9.cloned.1.call-start = ((), (), s32[]{:S(2)}) async-start(), calls=%async_computation.2 | async-start | bytes 1835008 | tf_op jit(solution)/shard_map/psum | solution.py:91
  568.1 329.9 %all-reduce.11.cloned.1.call-start = ((), (), s32[]{:S(2)}) async-start(), calls=%async_computation.3 | async-start | bytes 1835008 | tf_op jit(solution)/shard_map/psum | solution.py:91
  724.7 0.9 copy-start.4
Sparse Core Ops, SparseCore 0:
  25.8 42.7 all-gather.1
  157.2 100.9 all-reduce.12
  335.3 96.2 all-reduce.6
  568.3 95.8 all-reduce.8
  802.2 95.8 all-reduce.10
where the time goes:
time: 944 us; the launch traced here: 938 us
  waiting for transfers between devices  432 us (46%)
  blocking collectives  304 us (32%)
  matrix products  127 us (13%)
  other arithmetic  36.9 us (4%)
  between operations  21.2 us (2%)
  local copies, waits for them, and re-layouts  17.1 us (2%)
    psum x3, waiting for transfers between devices, local(): reduced = lax.psum(curvature_partial_value, 'view')  288 us
    psum x3, blocking collectives, local(): curvature_pixel_vec = lax.psum(partial_value, 'scene')  131 us
    psum x5, blocking collectives, inner_sum(): return lax.psum(local_sum, 'scene')  129 us
    psum x1, waiting for transfers between devices, local(): gradient, curv_diag = lax.psum((grad_part, diag_part), 'view')  101 us
    psum x1, blocking collectives, local(): render = lax.psum(render_part, 'scene')  43.5 us
    all_gather x1, waiting for transfers between devices, local(): all_logs = lax.all_gather(block_log, 'scene', axis=1, tiled=True)  42.5 us
    dot_general x4, matrix products, transpose_apply(): jnp.einsum('tcq,tjqg->ctjg', pixel_basis, slope_now * spread, precision=h...  40 us
    dot_general x3, matrix products, local(): jnp.einsum('tcq,ctjg->tjqg', pixel_basis, forward_pieces[:param_count - 1...  36.4 us
  transfers between devices with their start and end apart: 5, of which 5 were waited for; matrix products, arithmetic and copies ran while one was open for 0% of the time, Pallas kernels for 0%

commit v1 on v0

--- a/solution.py
+++ b/solution.py
@@ -9,6 +9,14 @@
 damping = 0.1
 ridge_term = 0.0001
 highest = lax.Precision.HIGHEST
+
+
+def added_up(x, axis):
+    size, result = (lax.axis_size(axis), x)
+    for far in [1 << k for k in range(size.bit_length() - 1)]:
+        swap = [(i, i ^ far) for i in range(size)]
+        result = result + lax.ppermute(result, axis, swap)
+    return result
 
 
 def local(params, pixel_basis, tile_blocks, depth_rank, target):
@@ -86,7 +94,7 @@
             slopes * projected + weight * forward_pieces[param_count - 1][:, :, None, :],
             axis=(1, 3),
         )
-        curvature_pixel_vec = lax.psum(partial_value, "scene")
+        curvature_pixel_vec = added_up(partial_value, "scene")
         curvature_partial_value = transpose_apply(weight, slopes, curvature_pixel_vec)
         reduced = lax.psum(curvature_partial_value, "view")
         image_dir = reduced + (damping * curv_diag + ridge_term) * direction

time: 944 us -> 852 us (0.903)
  blocking collectives: 304 us -> 172 us
  waiting for transfers between devices: 432 us -> 457 us
  starting transfers between devices: 0.42 us -> 23.8 us
  other arithmetic: 36.9 us -> 27.1 us
    psum x3 -> x0, blocking collectives: 131 us -> none  [local(): curvature_pixel_vec = lax.psum(partial_value, 'scene')]
    ppermute x0 -> x12, waiting for transfers between devices: none -> 24 us  [added_up(): result = result + lax.ppermute(result, axis, swap)]
    ppermute x0 -> x12, starting transfers between devices: none -> 23.3 us  [added_up(): result = result + lax.ppermute(result, axis, swap)]
    reduce_sum x4, other arithmetic: 16.1 us -> 6.11 us  [transpose_apply(): colour_term = jnp.sum(weight_now * spread, axis=2)]
  transfers between devices with their start and end apart: 5 -> 17, of which waited for: 5 -> 17; matrix products, arithmetic and copies ran while one was open for 0% -> 0% of each run, Pallas kernels for 0% -> 0%
where the time goes in v1:
time: 852 us; the launch traced here: 845 us
  waiting for transfers between devices  457 us (54%)
  blocking collectives  172 us (20%)
  matrix products  126 us (15%)
  other arithmetic  27.1 us (3%)
  starting transfers between devices  23.8 us (3%)
  between operations  21.2 us (2%)
  local copies, waits for them, and re-layouts  17.2 us (2%)
    psum x3, waiting for transfers between devices, local(): reduced = lax.psum(curvature_partial_value, 'view')  290 us
    psum x5, blocking collectives, inner_sum(): return lax.psum(local_sum, 'scene')  129 us
    psum x1, waiting for transfers between devices, local(): gradient, curv_diag = lax.psum((grad_part, diag_part), 'view')  101 us
    psum x1, blocking collectives, local(): render = lax.psum(render_part, 'scene')  43.5 us
    all_gather x1, waiting for transfers between devices, local(): all_logs = lax.all_gather(block_log, 'scene', axis=1, tiled=True)  42.4 us
    dot_general x3, matrix products, local(): jnp.einsum('tcq,ctjg->tjqg', pixel_basis, forward_pieces[:param_count - 1...  40.3 us
    dot_general x4, matrix products, transpose_apply(): jnp.einsum('tcq,tjqg->ctjg', pixel_basis, slope_now * spread, precision=h...  35.5 us
    ppermute x12, waiting for transfers between devices, added_up(): result = result + lax.ppermute(result, axis, swap)  24 us
  transfers between devices with their start and end apart: 17, of which 17 were waited for; matrix products, arithmetic and copies ran while one was open for 0% of the time, Pallas kernels for 0%

profile of v1, /device:TPU:1, one launch (start us, length us, event | category | flops | bytes accessed | tf_op | source)
XLA Modules:
  0.0 845.4 jit_solution(5751626245685515046)
XLA Ops:
  11.0 14.0 %fusion.19 = (f32[32,2,256]{2,1,0:T(2,128)S(1)}, f32[32,2,128,256]{3,2,1,0:T(8,128)}) fusion(f32[13,32,2,128]{3,0,2,1:T(8,128)S(1)} %bitcast.150, f32[32,13,256,1]{2,0,1,3:T(8,128)} %bitcast.130), kind=kOutput, calls=%fused_computation.35 | convolution fusion | flops 339722240 | bytes 9306112 | tf_op jit(solution)/shard_map/tcq,ctjg->tjqg/dot_general | solution.py:37
  26.2 42.4 %all-gather.2.cloned.1.call-done = f32[32,32,256]{2,0,1:T(8,128)} async-done(((f32[32,2,256]{2,0,1:T(8,128)}), f32[32,32,256]{2,0,1:T(8,128)}) %all-gather.2.cloned.1.call-update) | async-done | bytes 1048592 | tf_op jit(solution)/shard_map/all_gather | solution.py:43
  70.8 18.9 %bitcast_multiply_fusion.3 = (f32[32,2,256,128]{2,3,1,0:T(8,128)}, f32[32,256]{1,0:T(8,128)S(1)}, f32[32,2,256,128]{2,3,1,0:T(8,128)}) fusion(f32[32,2,128,256]{3,2,1,0:T(8,128)} %get-tuple-element.14, f32[32,2,128]{2,1,0:T(2,128)S(1)} %bitcast.156, f32[32,2,256]{2,1,0:T(2,128)S(1)} %fusion.27), kind=kOutput, calls=%fused_computation.13 | convolution fusion | flops 3240108032 | bytes 25296896 | tf_op jit(solution)/shard_map/tjqg,gh->tjqh/dot_general | solution.py:40
  89.7 43.5 %psum.84 = f32[32,256]{1,0:T(8,128)S(1)} all-reduce(f32[32,256]{1,0:T(8,128)S(1)} %get-tuple-element.12), channel_id=1, replica_groups=mesh['view'=16,'scene'=16] {'scene'}, use_global_device_ids=true, to_apply=%region_2.4 | all-reduce | flops 8192 | bytes 65536 | tf_op jit(solution)/shard_map/psum | solution.py:54
  133.3 10.5 %fusion.15 = f32[32,2,128,13]{2,3,1,0:T(8,128)S(1)} fusion(f32[32,2,256,128]{2,3,1,0:T(8,128)} %get-tuple-element.11, f32[32,256]{1,0:T(8,128)S(1)} %sub.13, f32[32,13,256,1]{2,0,1,3:T(8,128)S(1)} %bitcast.131), kind=kOutput, calls=%fused_computation.30 | convolution fusion | flops 329252864 | bytes 9273344 | tf_op jit(solution)/shard_map/tcq,tjqg->ctjg/dot_general | solution.py:64
  146.4 7.5 fusion.13
  157.3 101.0 %all-reduce.13.cloned.1.call-done = (f32[14,128,128]{2,1,0:T(8,128)}, f32[14,128,128]{2,1,0:T(8,128)}) async-done(((f32[14,128,128]{2,1,0:T(8,128)}, f32[14,128,128]{2,1,0:T(8,128)}), (f32[14,128,128]{2,1,0:T(8,128)}, f32[14,128,128]{2,1,0:T(8,128)})) %all-reduce.13.cloned.1.call-update) | async-done | bytes 1835024 | tf_op jit(solution)/shard_map/psum | solution.py:73
  261.3 12.5 %fusion.5 = f32[32,256]{1,0:T(8,128)S(1)} fusion(f32[32,2,256,128]{2,3,1,0:T(8,128)} %get-tuple-element.11, f32[32,2,256,128]{2,3,1,0:T(8,128)} %get-tuple-element.15, f32[32,2,128]{2,1,0:T(2,128)S(1)} %bitcast.157, f32[13,32,2,128]{3,0,2,1:T(8,128)S(1)} %bitcast.141, f32[32,13,256,1]{2,0,1,3:T(8,128)S(1)} %bitcast.132), kind=kOutput, calls=%fused_computation.12 | convolution fusion | flops 335536128 | bytes 17694720 | tf_op jit(solution)/shard_map/tcq,ctjg->tjqg/dot_general | solution.py:90
  283.5 6.0 collective-permute-start.3
  290.9 7.6 fusion.11
  301.6 97.6 %all-reduce.7.cloned.1.call-done = f32[14,128,128]{2,1,0:T(8,128)} async-done(((f32[14,128,128]{2,1,0:T(8,128)}), f32[14,128,128]{2,1,0:T(8,128)}) %all-reduce.7.cloned.1.call-update) | async-done | bytes 917520 | tf_op jit(solution)/shard_map/psum | solution.py:99
  401.4 26.2 %all-reduce = (f32[]{:T(128)}, f32[]{:T(128)}) all-reduce(f32[]{:T(128)} %get-tuple-element.6, f32[]{:T(128)} %get-tuple-element.5), channel_id=1, replica_groups=mesh['view'=16,'scene'=16] {'scene'}, use_global_device_ids=true, to_apply=%region_8.10 | all-reduce | flops 2 | bytes 16 | tf_op jit(solution)/shard_map/psum | solution.py:77
  431.3 25.2 %psum.90 = f32[]{:T(128)} all-reduce(f32[]{:T(128)} %multiply_reduce_fusion.9), channel_id=1, replica_groups=mesh['view'=16,'scene'=16] {'scene'}, use_global_device_ids=true, to_apply=%region_15.17 | all-reduce | flops 1 | bytes 8 | tf_op jit(solution)/shard_map/psum | solution.py:77
  460.8 2.6 gather_fusion.2
  464.9 13.9 %fusion.3 = f32[32,256]{1,0:T(8,128)S(1)} fusion(f32[32,2,256,128]{2,3,1,0:T(8,128)} %get-tuple-element.11, f32[32,2,256,128]{2,3,1,0:T(8,128)} %get-tuple-element.15, f32[32,2,128]{2,1,0:T(2,128)S(1)} %bitcast.158, f32[13,32,2,128]{3,0,2,1:T(8,128)S(1)} %bitcast.142, f32[32,13,256,1]{2,0,1,3:T(8,128)S(1)} %bitcast.134), kind=kOutput, calls=%fused_computation.9 | convolution fusion | flops 335536128 | bytes 17694720 | tf_op jit(solution)/shard_map/tcq,ctjg->tjqg/dot_general | solution.py:90
  480.4 2.8 collective-permute-done.5
  483.6 3.3 collective-permute-done.6
  486.9 4.7 collective-permute-start.7
  494.1 7.6 fusion.9
  504.7 96.2 %all-reduce.9.cloned.1.call-done = f32[14,128,128]{2,1,0:T(8,128)} async-done(((f32[14,128,128]{2,1,0:T(8,128)}), f32[14,128,128]{2,1,0:T(8,128)}) %all-reduce.9.cloned.1.call-update) | async-done | bytes 917520 | tf_op jit(solution)/shard_map/psum | solution.py:99
  602.9 26.2 %psum.92 = f32[]{:T(128)} all-reduce(f32[]{:T(128)} %multiply_reduce_fusion.8), channel_id=1, replica_groups=mesh['view'=16,'scene'=16] {'scene'}, use_global_device_ids=true, to_apply=%region_20.22 | all-reduce | flops 1 | bytes 8 | tf_op jit(solution)/shard_map/psum | solution.py:77
  630.3 2.6 multiply_reduce_fusion.7
  632.9 25.2 %psum.93 = f32[]{:T(128)} all-reduce(f32[]{:T(128)} %multiply_reduce_fusion.7), channel_id=1, replica_groups=mesh['view'=16,'scene'=16] {'scene'}, use_global_device_ids=true, to_apply=%region_22.24 | all-reduce | flops 1 | bytes 8 | tf_op jit(solution)/shard_map/psum | solution.py:77
  663.8 2.6 gather_fusion.3
  667.7 13.9 %fusion.1 = f32[32,256]{1,0:T(8,128)S(1)} fusion(f32[32,2,256,128]{2,3,1,0:T(8,128)} %get-tuple-element.11, f32[32,2,256,128]{2,3,1,0:T(8,128)} %get-tuple-element.15, f32[32,2,128]{2,1,0:T(2,128)S(1)} %bitcast.159, f32[13,32,2,128]{3,0,2,1:T(8,128)S(1)} %bitcast.140, f32[32,13,256,1]{2,0,1,3:T(8,128)S(1)} %bitcast.136), kind=kOutput, calls=%fused_computation.6 | convolution fusion | flops 335536128 | bytes 17694720 | tf_op jit(solution)/shard_map/tcq,ctjg->tjqg/dot_general | solution.py:90
  683.2 2.8 collective-permute-done.9
  686.4 3.4 collective-permute-done.10
  689.7 4.4 collective-permute-start.11
  694.2 2.4 collective-permute-done.11
  696.6 9.8 %fusion.7 = f32[32,2,128,13]{2,3,1,0:T(8,128)S(1)} fusion(f32[32,2,256,128]{2,3,1,0:T(8,128)} %get-tuple-element.11, f32[32,256]{1,0:T(8,128)S(1)} %add.144, f32[32,13,256,1]{2,0,1,3:T(8,128)S(1)} %bitcast.137), kind=kOutput, calls=%fused_computation.18 | convolution fusion | flops 329252864 | bytes 9273344 | tf_op jit(solution)/shard_map/tcq,tjqg->ctjg/dot_general | solution.py:64
  709.4 96.2 %all-reduce.11.cloned.1.call-done = f32[14,128,128]{2,1,0:T(8,128)} async-done(((f32[14,128,128]{2,1,0:T(8,128)}), f32[14,128,128]{2,1,0:T(8,128)}) %all-reduce.11.cloned.1.call-update) | async-done | bytes 917520 | tf_op jit(solution)/shard_map/psum | solution.py:99
  807.9 26.2 %psum.95 = f32[]{:T(128)} all-reduce(f32[]{:T(128)} %multiply_reduce_fusion.6), channel_id=1, replica_groups=mesh['view'=16,'scene'=16] {'scene'}, use_global_device_ids=true, to_apply=%region_27.29 | all-reduce | flops 1 | bytes 8 | tf_op jit(solution)/shard_map/psum | solution.py:77
  (134 shorter events, 64.6 us)
Async XLA Ops:
  7.2 61.4 %all-gather.2.cloned.1.call-start = ((), (), s32[]{:S(2)}) async-start(), calls=%async_computation | async-start | bytes 1114112 | tf_op jit(solution)/shard_map/all_gather | solution.py:43
  11.0 15.1 %copy-start.6 = (s32[32,32]{1,0:T(8,128)S(1)}, s32[32,32]{1,0:T(8,128)}, u32[]{:S(2)}) copy-start(s32[32,32]{1,0:T(8,128)} %param.10) | copy-start | bytes 12292
  11.0 15.2 %copy-start.3 = (f32[32,13,256]{2,0,1:T(8,128)S(1)}, f32[32,13,256]{2,0,1:T(8,128)}, u32[]{:S(2)}) copy-start(f32[32,13,256]{2,0,1:T(8,128)} %param.8) | copy-start | bytes 1277956
  25.7 232.6 %all-reduce.13.cloned.1.call-start = ((), (), s32[]{:S(2)}) async-start(), calls=%async_computation.4 | async-start | bytes 3670016 | tf_op jit(solution)/shard_map/psum | solution.py:73
  70.8 62.5 %copy-start.7 = (f32[32,256]{1,0:T(8,128)S(1)}, f32[32,256]{1,0:T(8,128)}, u32[]{:S(2)}) copy-start(f32[32,256]{1,0:T(8,128)} %param.11) | copy-start | bytes 98308
  157.2 242.0 %all-reduce.7.cloned.1.call-start = ((), (), s32[]{:S(2)}) async-start(), calls=%async_computation.1 | async-start | bytes 1835008 | tf_op jit(solution)/shard_map/psum | solution.py:99
  261.1 29.8 %slice-start.2 = ((s8[8388608]{0:T(1024)(128)(4,1)}), s8[4194304]{0:T(1024)(128)(4,1)S(1)}, s32[]{:S(2)}) async-start(s8[8388608]{0:T(1024)(128)(4,1)} %bitcast.120), calls=%async_computation.7 | async-start | bytes 8388608
  261.3 37.2 %slice-start.6 = ((s8[8388608]{0:T(1024)(128)(4,1)}), s8[4194304]{0:T(1024)(128)(4,1)S(1)}, s32[]{:S(2)}) async-start(s8[8388608]{0:T(1024)(128)(4,1)} %bitcast.124), calls=%async_computation.11 | async-start | bytes 8388608
  261.3 29.6 %slice-start.3 = ((s8[8388608]{0:T(1024)(128)(4,1)}), s8[4194304]{0:T(1024)(128)(4,1)S(1)}, s32[]{:S(2)}) async-start(s8[8388608]{0:T(1024)(128)(4,1)} %bitcast.120), calls=%async_computation.8 | async-start | bytes 8388608
  261.3 37.2 %slice-start.7 = ((s8[8388608]{0:T(1024)(128)(4,1)}), s8[4194304]{0:T(1024)(128)(4,1)S(1)}, s32[]{:S(2)}) async-start(s8[8388608]{0:T(1024)(128)(4,1)} %bitcast.124), calls=%async_computation.12 | async-start | bytes 8388608
  273.8 3.2 collective-permute-start
  277.1 2.8 collective-permute-start.1
  279.8 3.7 collective-permute-start.2
  283.5 7.4 collective-permute-start.3
  290.9 108.3 %copy-start.1 = (f32[14,128,128]{2,1,0:T(8,128)S(1)}, f32[14,128,128]{2,1,0:T(8,128)}, u32[]{:S(2)}) copy-start(f32[14,128,128]{2,1,0:T(8,128)} %get-tuple-element.9) | copy-start | bytes 2752516
  290.9 108.2 %copy-start.2 = (f32[14,128,128]{2,1,0:T(8,128)S(1)}, f32[14,128,128]{2,1,0:T(8,128)}, u32[]{:S(2)}) copy-start(f32[14,128,128]{2,1,0:T(8,128)} %get-tuple-element.10) | copy-start | bytes 2752516
  301.5 299.3 %all-reduce.9.cloned.1.call-start = ((), (), s32[]{:S(2)}) async-start(), calls=%async_computation.2 | async-start | bytes 1835008 | tf_op jit(solution)/shard_map/psum | solution.py:99
  463.4 30.6 %slice-start.4 = ((s8[8388608]{0:T(1024)(128)(4,1)}), s8[4194304]{0:T(1024)(128)(4,1)S(1)}, s32[]{:S(2)}) async-start(s8[8388608]{0:T(1024)(128)(4,1)} %bitcast.122), calls=%async_computation.9 | async-start | bytes 8388608
  464.8 36.8 %slice-start.8 = ((s8[8388608]{0:T(1024)(128)(4,1)}), s8[4194304]{0:T(1024)(128)(4,1)S(1)}, s32[]{:S(2)}) async-start(s8[8388608]{0:T(1024)(128)(4,1)} %bitcast.126), calls=%async_computation.13 | async-start | bytes 8388608
  464.8 29.2 %slice-start.5 = ((s8[8388608]{0:T(1024)(128)(4,1)}), s8[4194304]{0:T(1024)(128)(4,1)S(1)}, s32[]{:S(2)}) async-start(s8[8388608]{0:T(1024)(128)(4,1)} %bitcast.122), calls=%async_computation.10 | async-start | bytes 8388608
  464.8 36.8 %slice-start.9 = ((s8[8388608]{0:T(1024)(128)(4,1)}), s8[4194304]{0:T(1024)(128)(4,1)S(1)}, s32[]{:S(2)}) async-start(s8[8388608]{0:T(1024)(128)(4,1)} %bitcast.126), calls=%async_computation.14 | async-start | bytes 8388608
  478.8 1.6 collective-permute-start.4
  480.4 2.8 collective-permute-start.5
  483.2 3.7 collective-permute-start.6
  486.9 7.1 collective-permute-start.7
  504.6 301.0 %all-reduce.11.cloned.1.call-start = ((), (), s32[]{:S(2)}) async-start(), calls=%async_computation.3 | async-start | bytes 1835008 | tf_op jit(solution)/shard_map/psum | solution.py:99
  667.7 38.8 %slice-start.10 = ((s8[8388608]{0:T(1024)(128)(4,1)}), s8[4194304]{0:T(1024)(128)(4,1)S(1)}, s32[]{:S(2)}) async-start(s8[8388608]{0:T(1024)(128)(4,1)} %bitcast.128), calls=%async_computation.15 | async-start | bytes 8388608
  667.7 38.8 %slice-start.11 = ((s8[8388608]{0:T(1024)(128)(4,1)}), s8[4194304]{0:T(1024)(128)(4,1)S(1)}, s32[]{:S(2)}) async-start(s8[8388608]{0:T(1024)(128)(4,1)} %bitcast.128), calls=%async_computation.16 | async-start | bytes 8388608
  681.6 1.6 collective-permute-start.8
  683.2 2.8 collective-permute-start.9
  686.0 3.7 collective-permute-start.10
  689.7 6.9 collective-permute-start.11
  (5 other events, 50.9 us)
Sparse Core Ops, SparseCore 0:
  25.8 42.7 all-gather.1
  157.3 100.9 all-reduce.12
  301.6 97.4 all-reduce.6
  504.8 96.0 all-reduce.8
  709.6 95.9 all-reduce.10
